TPU v7x, 128 devices: a whole 4x4x4 slice. The times are simulated.
128 devices in a mesh: tm: 16 (over x, y), sector: 8 (over z, core).
Axes of the slice: x: 4, y: 4, z: 4, core: 2. Of those that a mesh axis runs over, the one named last changes fastest.
Arguments:
- propagator: bfloat16 [8, 16, 640, 640], P('sector', 'tm'), may hold values from -6 to 6
- rising_op: bfloat16 [8, 640, 640], P('sector'), may hold values from -0.25 to 0.25
- energies: float32 [8, 640], P('sector'), may hold values from 0.5 to 40
- hyb_particle: float32 [16], P('tm'), may hold values from 0.2 to 1
- hyb_hole: float32 [16], P('tm'), may hold values from 0.2 to 1
- sector_sizes: int32 [8], P('sector'), may hold values from 160 to 640, as said below
Outputs:
- new_prop: bfloat16 [8, 16, 640, 640], P('sector', 'tm')
Inputs may be any that keep to these rules, and one draw needn't show every extreme that they name: `sector_sizes`: one sector holds exactly 640 states.
All inputs are finite; a program needn't handle non-finite values.
Results may differ from a plain program's by a relative error of at most 0.0061.
Values may be sent and summed in bfloat16 or wider, within the bound.
No kernel may reach another device: no remote copies, remote signals or barrier semaphores. Data moves between devices by JAX's collectives and lax.ppermute only.
A program may use at most 128 MiB of HBM per device.

v0:
```python
import jax
import jax.numpy as jnp
from jax import lax
from jax.sharding import PartitionSpec as P


def shifted(block, axis, distance):
    devices = range(lax.axis_size(axis))
    route = [(i - distance, i) for i in devices if i - distance in devices]
    return lax.ppermute(block, axis, route)


def split_up(value, dim, size):
    before, after = (value.shape[:dim], value.shape[dim + 1 :])
    return jnp.moveaxis(value.reshape(*before, size, -1, *after), dim, 0)


def piece_ends(length, count):
    step = length // count
    if step >= 8:
        step -= step % 8
    return [step * k for k in range(1, count)]


def laid_out(pieces, dim):
    dims = list(pieces.shape[1:])
    dims[dim] *= pieces.shape[0]
    return jnp.moveaxis(pieces, 0, dim).reshape(dims)


def several_exchanges(value, axis, pieces, split_dim, concat_dim):
    blocks = split_up(value, split_dim, lax.axis_size(axis))
    cut = max(range(1, max(2, blocks.ndim - 1)), key=lambda d: blocks.shape[d])
    finished = []
    for share in jnp.split(blocks, piece_ends(blocks.shape[cut], pieces), axis=cut):
        if share.size:
            finished.append(lax.all_to_all(share, axis, split_axis=0, concat_axis=0, tiled=True))
    return laid_out(jnp.concatenate(finished, axis=cut), concat_dim)


def per_device(propagator, rising_op, energies, hyb_particle, hyb_hole, sector_sizes):
    t_dev = propagator.shape[1]
    states = propagator.shape[2]
    time_count = t_dev * lax.axis_size("tm")
    step_size = 1.0 / time_count
    positions = jnp.arange(states, dtype=jnp.int32)
    live_mask = positions < sector_sizes[0]
    square = live_mask[:, None] & live_mask[None, :]
    masked_prop = jnp.where(square[None], propagator[0], jnp.zeros((), jnp.bfloat16))
    operator = rising_op[0]
    raised = jnp.einsum(
        "ik,tkl->til", operator, masked_prop, preferred_element_type=jnp.float32
    ).astype(jnp.bfloat16)
    upward = jnp.einsum("tik,jk->tij", raised, operator, preferred_element_type=jnp.float32).astype(
        jnp.bfloat16
    )
    from_below = shifted(upward, "sector", 1)
    from_above = shifted(masked_prop, "sector", -1)
    lowered = jnp.einsum(
        "ki,tkl->til", operator, from_above, preferred_element_type=jnp.float32
    ).astype(jnp.bfloat16)
    downward = jnp.einsum("tik,kl->til", lowered, operator, preferred_element_type=jnp.float32)
    combined = (
        hyb_particle[:, None, None] * from_below.astype(jnp.float32)
        + hyb_hole[:, None, None] * downward
    )
    self_energy = jnp.where(square[None], combined, jnp.zeros((), jnp.float32)).astype(jnp.bfloat16)
    rows_each = states // lax.axis_size("tm")
    first_row = lax.axis_index("tm") * rows_each
    lag_rows = several_exchanges(self_energy, "tm", 2, 1, 0)
    history = lax.all_gather(masked_prop, "tm", axis=0, tiled=True)
    mirrored = jnp.concatenate([history[::-1], history], 0)
    slots = jnp.arange(time_count, dtype=jnp.int32)
    wide_slots = jnp.arange(time_count + 1, dtype=jnp.int32)

    def pair_step(lag, sums):
        forward, backward = sums
        other = time_count - 1 - lag
        window = lax.dynamic_slice_in_dim(mirrored, lag, time_count + 1, 0)
        near = lax.dynamic_index_in_dim(lag_rows, lag, 0, keepdims=False)
        far = lax.dynamic_index_in_dim(lag_rows, other, 0, keepdims=False)
        left = jnp.where((wide_slots < time_count - lag)[:, None, None], near[None], far[None])
        product = jnp.einsum("uik,ukl->uil", left, window, preferred_element_type=jnp.float32)
        backward = backward + jnp.where(
            (slots < time_count - lag)[:, None, None],
            product[:time_count],
            jnp.zeros((), jnp.float32),
        )
        forward = forward + jnp.where(
            (slots >= time_count - lag - 1)[:, None, None], product[1:], jnp.zeros((), jnp.float32)
        )
        return (forward, backward)

    empty_rows = jnp.zeros((time_count, rows_each, states), jnp.float32)
    forward, backward = lax.fori_loop(0, time_count // 2, pair_step, (empty_rows, empty_rows))
    convolved = step_size * (forward + backward[::-1])
    row_ids = first_row + jnp.arange(rows_each, dtype=jnp.int32)
    row_rates = lax.dynamic_slice_in_dim(energies[0], first_row, rows_each, 0)
    decay_rows = jnp.exp(-step_size * row_rates)

    def advance(running, term):
        running = decay_rows[:, None] * running + term
        return (running, running)

    _, summed = lax.scan(advance, jnp.zeros((rows_each, states), jnp.float32), convolved)
    moments = jnp.arange(time_count).astype(jnp.float32) * step_size
    live_rows = row_ids < sector_sizes[0]
    free_part = jnp.where(
        live_rows[None, :],
        jnp.exp(-row_rates[None, :] * moments[:, None]),
        jnp.zeros((), jnp.float32),
    )
    diagonal = jnp.where(
        (row_ids[:, None] == positions[None, :])[None],
        free_part[:, :, None],
        jnp.zeros((), jnp.float32),
    )
    new_rows = (diagonal - step_size * summed).astype(jnp.bfloat16)
    return lax.all_to_all(new_rows, "tm", split_axis=0, concat_axis=1, tiled=True)[None]


def solution(mesh):
    placed = (
        P("sector", "tm", None, None),
        P("sector", None, None),
        P("sector", None),
        P("tm"),
        P("tm"),
        P("sector"),
    )
    return jax.shard_map(
        per_device,
        mesh=mesh,
        in_specs=placed,
        out_specs=P("sector", "tm", None, None),
        check_vma=False,
    )
```

profile of v0, /device:TPU:32, one launch (start us, length us, event | category | flops | bytes accessed | tf_op | source)
XLA Modules:
  0.0 278.3 jit_solution(17964893264941335905)
XLA Ops:
  7.3 2.4 and_select_fusion.1
  9.7 1.9 collective-permute-start.1
  11.7 2.9 %fusion.15 = bf16[1,640,640]{2,1,0:T(8,128)(2,1)} fusion(bf16[1,1,640,640]{3,2,1,0:T(8,128)(2,1)S(1)} %copy-done.2, bf16[1,640,640]{2,1,0:T(8,128)(2,1)S(1)} %copy-done, pred[640]{0:T(1024)(128)(4,1)S(1)} %iota_compare_fusion.4), kind=kOutput, calls=%fused_computation.33 | convolution fusion | flops 1050214400 | bytes 2458240 | tf_op jit(solution)/shard_map/tik,jk->tij/dot_general | solution.py:54
  14.6 2.4 collective-permute-start
  18.3 3.6 %collective-permute-done.1 = bf16[1,640,640]{2,1,0:T(8,128)(2,1)S(1)} collective-permute-done((bf16[1,640,640]{2,1,0:T(8,128)(2,1)}, bf16[1,640,640]{2,1,0:T(8,128)(2,1)S(1)}, u32[]{:S(2)}, u32[]{:S(2)}) %collective-permute-start.1) | collective-permute-done | bytes 819232 | tf_op jit(solution)/shard_map/ppermute | solution.py:10
  21.8 6.6 %collective-permute-done = bf16[1,640,640]{2,1,0:T(8,128)(2,1)S(1)} collective-permute-done((bf16[1,640,640]{2,1,0:T(8,128)(2,1)}, bf16[1,640,640]{2,1,0:T(8,128)(2,1)S(1)}, u32[]{:S(2)}, u32[]{:S(2)}) %collective-permute-start) | collective-permute-done | bytes 819232 | tf_op jit(solution)/shard_map/ppermute | solution.py:10
  29.3 3.5 %fusion.13 = bf16[1,640,640]{2,1,0:T(8,128)(2,1)S(1)} fusion(bf16[1,640,640]{2,1,0:T(8,128)(2,1)} %copy-done.3, bf16[1,640,640]{2,1,0:T(8,128)(2,1)S(1)} %collective-permute-done.1, bf16[1,640,640]{2,1,0:T(8,128)(2,1)S(1)} %copy-done, f32[]{:T(128)} %bitcast.67, f32[]{:T(128)} %bitcast.66, pred[640]{0:T(1024)(128)(4,1)S(1)} %iota_compare_fusion.4), kind=kOutput, calls=%fused_computation.24 | convolution fusion | flops 1051852800 | bytes 3277448 | tf_op jit(solution)/shard_map/tik,kl->til/dot_general | solution.py:62
  33.5 7.0 %all-to-all-start = ((bf16[16,1,16,640]{3,2,1,0:T(8,128)(2,1)}), bf16[16,1,16,640]{3,2,1,0:T(8,128)(2,1)S(1)}, u32[]{:S(2)}, u32[]{:S(2)}) async-start(bf16[16,1,16,640]{3,2,1,0:T(8,128)(2,1)} %split.8), calls=%async_computation | async-start | bytes 655360 | tf_op jit(solution)/shard_map/all_to_all | solution.py:37
  42.2 7.4 %all-to-all-done = bf16[16,1,16,640]{3,2,1,0:T(8,128)(2,1)S(1)} async-done(((bf16[16,1,16,640]{3,2,1,0:T(8,128)(2,1)}), bf16[16,1,16,640]{3,2,1,0:T(8,128)(2,1)S(1)}, u32[]{:S(2)}, u32[]{:S(2)}) %all-to-all-start) | async-done | bytes 327712 | tf_op jit(solution)/shard_map/all_to_all | solution.py:37
  49.6 3.7 %all-to-all-start.1 = ((bf16[16,1,24,640]{3,2,1,0:T(8,128)(2,1)}), bf16[16,1,24,640]{3,2,1,0:T(8,128)(2,1)S(1)}, u32[]{:S(2)}, u32[]{:S(2)}) async-start(bf16[16,1,24,640]{3,2,1,0:T(8,128)(2,1)} %split.9), calls=%async_computation.1 | async-start | bytes 983040 | tf_op jit(solution)/shard_map/all_to_all | solution.py:37
  53.5 14.7 %all-to-all-done.1 = bf16[16,1,24,640]{3,2,1,0:T(8,128)(2,1)S(1)} async-done(((bf16[16,1,24,640]{3,2,1,0:T(8,128)(2,1)}), bf16[16,1,24,640]{3,2,1,0:T(8,128)(2,1)S(1)}, u32[]{:S(2)}, u32[]{:S(2)}) %all-to-all-start.1) | async-done | bytes 491552 | tf_op jit(solution)/shard_map/all_to_all | solution.py:37
  68.2 42.9 %all-gather.2.cloned.1.call-done = bf16[16,640,640]{2,1,0:T(8,128)(2,1)} async-done(((bf16[1,640,640]{2,1,0:T(8,128)(2,1)}), bf16[16,640,640]{2,1,0:T(8,128)(2,1)}) %all-gather.2.cloned.1.call-update) | async-done | bytes 13107216 | tf_op jit(solution)/shard_map/all_gather | solution.py:71
  111.1 10.8 %rev.6 = bf16[16,640,640]{2,1,0:T(8,128)(2,1)} reverse(bf16[16,640,640]{2,1,0:T(8,128)(2,1)} %all-gather.2.cloned.1.call-done), dimensions={0} | reverse | bytes 26214400 | tf_op jit(solution)/shard_map/rev | solution.py:72
  122.0 18.6 %pad_maximum_fusion = bf16[32,640,640]{2,1,0:T(8,128)(2,1)} fusion(bf16[16,640,640]{2,1,0:T(8,128)(2,1)} %all-gather.2.cloned.1.call-done, bf16[16,640,640]{2,1,0:T(8,128)(2,1)} %rev.6), kind=kLoop, calls=%fused_computation.21 | loop fusion | flops 13107200 | bytes 52428800 | tf_op jit(solution)/shard_map/concatenate | solution.py:72
  140.6 90.8 %while.35 = (s32[]{:T(128)}, f32[16,40,640]{2,1,0:T(8,128)}, f32[16,40,640]{2,1,0:T(8,128)}, bf16[16,40,640]{2,1,0:T(8,128)(2,1)S(1)}, bf16[32,640,640]{2,1,0:T(...) while((s32[]{:T(128)}, f32[16,40,640]{2,1,0:T(8,128)}, ...), condition=%wide.region_1.2_spmd.clone.clone, body=%wide.region_0.1_spmd.clone.clone.sunk | while | flops 559948800 | bytes 25805600 | solution.py:95
  140.6 7.3 %fusion.40 = f32[17,40,640]{2,1,0:T(8,128)S(1)} fusion(bf16[32,640,640]{2,1,0:T(8,128)(2,1)} %get-tuple-element.458, s32[]{:T(128)} %get-tuple-element.444, pred[17]{0:T(512)(128)(4,1)S(1)} %iota_compare_fusion.7, bf16[40,640]{1,0:T(8,128)(2,1)S(1)} %get-tuple-element.428, bf16[40,640]{1,0:T(8,128)(2,1)S(1)} %get-tuple-element.429), kind=kOutput, calls=%fused_computation.5.clone.1 | convolution fusion | flops 557491200 | bytes 15770129 | tf_op jit(solution)/shard_map/while/body/eval_jaxpr/uik,ukl->uil/dot_general | solution.py:83
  148.0 2.3 fusion.41
  150.3 7.3 %fusion.40 = f32[17,40,640]{2,1,0:T(8,128)S(1)} fusion(bf16[32,640,640]{2,1,0:T(8,128)(2,1)} %get-tuple-element.458, s32[]{:T(128)} %get-tuple-element.444, pred[17]{0:T(512)(128)(4,1)S(1)} %iota_compare_fusion.7, bf16[40,640]{1,0:T(8,128)(2,1)S(1)} %get-tuple-element.428, bf16[40,640]{1,0:T(8,128)(2,1)S(1)} %get-tuple-element.429), kind=kOutput, calls=%fused_computation.5.clone.1 | convolution fusion | flops 557491200 | bytes 15770129 | tf_op jit(solution)/shard_map/while/body/eval_jaxpr/uik,ukl->uil/dot_general | solution.py:83
  157.6 4.2 %fusion.41 = (f32[16,40,640]{2,1,0:T(8,128)}, f32[16,40,640]{2,1,0:T(8,128)}) fusion(f32[17,40,640]{2,1,0:T(8,128)S(1)} %fusion.40, f32[16,40,640]{2,1,0:T(8,128)} %get-tuple-element.446, pred[16]{0:T(512)(128)(4,1)S(1)} %get-tuple-element.430, pred[]{:T(512)S(6)} %compare.7, pred[16]{0:T(512)(128)(4,1)S(1)} %get-tuple-element.431, ...), kind=kLoop, calls=%fused_computation.8.clone.1 | loop fusion | flops 2457600 | bytes 9830433 | tf_op jit(solution)/shard_map/while/body/eval_jaxpr/add | solution.py:84
  161.9 7.3 %fusion.40 = f32[17,40,640]{2,1,0:T(8,128)S(1)} fusion(bf16[32,640,640]{2,1,0:T(8,128)(2,1)} %get-tuple-element.458, s32[]{:T(128)} %get-tuple-element.444, pred[17]{0:T(512)(128)(4,1)S(1)} %iota_compare_fusion.7, bf16[40,640]{1,0:T(8,128)(2,1)S(1)} %get-tuple-element.428, bf16[40,640]{1,0:T(8,128)(2,1)S(1)} %get-tuple-element.429), kind=kOutput, calls=%fused_computation.5.clone.1 | convolution fusion | flops 557491200 | bytes 15770129 | tf_op jit(solution)/shard_map/while/body/eval_jaxpr/uik,ukl->uil/dot_general | solution.py:83
  169.2 4.2 %fusion.41 = (f32[16,40,640]{2,1,0:T(8,128)}, f32[16,40,640]{2,1,0:T(8,128)}) fusion(f32[17,40,640]{2,1,0:T(8,128)S(1)} %fusion.40, f32[16,40,640]{2,1,0:T(8,128)} %get-tuple-element.446, pred[16]{0:T(512)(128)(4,1)S(1)} %get-tuple-element.430, pred[]{:T(512)S(6)} %compare.7, pred[16]{0:T(512)(128)(4,1)S(1)} %get-tuple-element.431, ...), kind=kLoop, calls=%fused_computation.8.clone.1 | loop fusion | flops 2457600 | bytes 9830433 | tf_op jit(solution)/shard_map/while/body/eval_jaxpr/add | solution.py:84
  173.5 7.3 %fusion.40 = f32[17,40,640]{2,1,0:T(8,128)S(1)} fusion(bf16[32,640,640]{2,1,0:T(8,128)(2,1)} %get-tuple-element.458, s32[]{:T(128)} %get-tuple-element.444, pred[17]{0:T(512)(128)(4,1)S(1)} %iota_compare_fusion.7, bf16[40,640]{1,0:T(8,128)(2,1)S(1)} %get-tuple-element.428, bf16[40,640]{1,0:T(8,128)(2,1)S(1)} %get-tuple-element.429), kind=kOutput, calls=%fused_computation.5.clone.1 | convolution fusion | flops 557491200 | bytes 15770129 | tf_op jit(solution)/shard_map/while/body/eval_jaxpr/uik,ukl->uil/dot_general | solution.py:83
  180.8 4.2 %fusion.41 = (f32[16,40,640]{2,1,0:T(8,128)}, f32[16,40,640]{2,1,0:T(8,128)}) fusion(f32[17,40,640]{2,1,0:T(8,128)S(1)} %fusion.40, f32[16,40,640]{2,1,0:T(8,128)} %get-tuple-element.446, pred[16]{0:T(512)(128)(4,1)S(1)} %get-tuple-element.430, pred[]{:T(512)S(6)} %compare.7, pred[16]{0:T(512)(128)(4,1)S(1)} %get-tuple-element.431, ...), kind=kLoop, calls=%fused_computation.8.clone.1 | loop fusion | flops 2457600 | bytes 9830433 | tf_op jit(solution)/shard_map/while/body/eval_jaxpr/add | solution.py:84
  185.1 7.3 %fusion.40 = f32[17,40,640]{2,1,0:T(8,128)S(1)} fusion(bf16[32,640,640]{2,1,0:T(8,128)(2,1)} %get-tuple-element.458, s32[]{:T(128)} %get-tuple-element.444, pred[17]{0:T(512)(128)(4,1)S(1)} %iota_compare_fusion.7, bf16[40,640]{1,0:T(8,128)(2,1)S(1)} %get-tuple-element.428, bf16[40,640]{1,0:T(8,128)(2,1)S(1)} %get-tuple-element.429), kind=kOutput, calls=%fused_computation.5.clone.1 | convolution fusion | flops 557491200 | bytes 15770129 | tf_op jit(solution)/shard_map/while/body/eval_jaxpr/uik,ukl->uil/dot_general | solution.py:83
  192.4 4.2 %fusion.41 = (f32[16,40,640]{2,1,0:T(8,128)}, f32[16,40,640]{2,1,0:T(8,128)}) fusion(f32[17,40,640]{2,1,0:T(8,128)S(1)} %fusion.40, f32[16,40,640]{2,1,0:T(8,128)} %get-tuple-element.446, pred[16]{0:T(512)(128)(4,1)S(1)} %get-tuple-element.430, pred[]{:T(512)S(6)} %compare.7, pred[16]{0:T(512)(128)(4,1)S(1)} %get-tuple-element.431, ...), kind=kLoop, calls=%fused_computation.8.clone.1 | loop fusion | flops 2457600 | bytes 9830433 | tf_op jit(solution)/shard_map/while/body/eval_jaxpr/add | solution.py:84
  196.7 7.3 %fusion.40 = f32[17,40,640]{2,1,0:T(8,128)S(1)} fusion(bf16[32,640,640]{2,1,0:T(8,128)(2,1)} %get-tuple-element.458, s32[]{:T(128)} %get-tuple-element.444, pred[17]{0:T(512)(128)(4,1)S(1)} %iota_compare_fusion.7, bf16[40,640]{1,0:T(8,128)(2,1)S(1)} %get-tuple-element.428, bf16[40,640]{1,0:T(8,128)(2,1)S(1)} %get-tuple-element.429), kind=kOutput, calls=%fused_computation.5.clone.1 | convolution fusion | flops 557491200 | bytes 15770129 | tf_op jit(solution)/shard_map/while/body/eval_jaxpr/uik,ukl->uil/dot_general | solution.py:83
  204.0 4.2 %fusion.41 = (f32[16,40,640]{2,1,0:T(8,128)}, f32[16,40,640]{2,1,0:T(8,128)}) fusion(f32[17,40,640]{2,1,0:T(8,128)S(1)} %fusion.40, f32[16,40,640]{2,1,0:T(8,128)} %get-tuple-element.446, pred[16]{0:T(512)(128)(4,1)S(1)} %get-tuple-element.430, pred[]{:T(512)S(6)} %compare.7, pred[16]{0:T(512)(128)(4,1)S(1)} %get-tuple-element.431, ...), kind=kLoop, calls=%fused_computation.8.clone.1 | loop fusion | flops 2457600 | bytes 9830433 | tf_op jit(solution)/shard_map/while/body/eval_jaxpr/add | solution.py:84
  208.2 7.3 %fusion.40 = f32[17,40,640]{2,1,0:T(8,128)S(1)} fusion(bf16[32,640,640]{2,1,0:T(8,128)(2,1)} %get-tuple-element.458, s32[]{:T(128)} %get-tuple-element.444, pred[17]{0:T(512)(128)(4,1)S(1)} %iota_compare_fusion.7, bf16[40,640]{1,0:T(8,128)(2,1)S(1)} %get-tuple-element.428, bf16[40,640]{1,0:T(8,128)(2,1)S(1)} %get-tuple-element.429), kind=kOutput, calls=%fused_computation.5.clone.1 | convolution fusion | flops 557491200 | bytes 15770129 | tf_op jit(solution)/shard_map/while/body/eval_jaxpr/uik,ukl->uil/dot_general | solution.py:83
  215.6 4.2 %fusion.41 = (f32[16,40,640]{2,1,0:T(8,128)}, f32[16,40,640]{2,1,0:T(8,128)}) fusion(f32[17,40,640]{2,1,0:T(8,128)S(1)} %fusion.40, f32[16,40,640]{2,1,0:T(8,128)} %get-tuple-element.446, pred[16]{0:T(512)(128)(4,1)S(1)} %get-tuple-element.430, pred[]{:T(512)S(6)} %compare.7, pred[16]{0:T(512)(128)(4,1)S(1)} %get-tuple-element.431, ...), kind=kLoop, calls=%fused_computation.8.clone.1 | loop fusion | flops 2457600 | bytes 9830433 | tf_op jit(solution)/shard_map/while/body/eval_jaxpr/add | solution.py:84
  219.8 7.3 %fusion.40 = f32[17,40,640]{2,1,0:T(8,128)S(1)} fusion(bf16[32,640,640]{2,1,0:T(8,128)(2,1)} %get-tuple-element.458, s32[]{:T(128)} %get-tuple-element.444, pred[17]{0:T(512)(128)(4,1)S(1)} %iota_compare_fusion.7, bf16[40,640]{1,0:T(8,128)(2,1)S(1)} %get-tuple-element.428, bf16[40,640]{1,0:T(8,128)(2,1)S(1)} %get-tuple-element.429), kind=kOutput, calls=%fused_computation.5.clone.1 | convolution fusion | flops 557491200 | bytes 15770129 | tf_op jit(solution)/shard_map/while/body/eval_jaxpr/uik,ukl->uil/dot_general | solution.py:83
  227.1 4.2 %fusion.41 = (f32[16,40,640]{2,1,0:T(8,128)}, f32[16,40,640]{2,1,0:T(8,128)}) fusion(f32[17,40,640]{2,1,0:T(8,128)S(1)} %fusion.40, f32[16,40,640]{2,1,0:T(8,128)} %get-tuple-element.446, pred[16]{0:T(512)(128)(4,1)S(1)} %get-tuple-element.430, pred[]{:T(512)S(6)} %compare.7, pred[16]{0:T(512)(128)(4,1)S(1)} %get-tuple-element.431, ...), kind=kLoop, calls=%fused_computation.8.clone.1 | loop fusion | flops 2457600 | bytes 9830433 | tf_op jit(solution)/shard_map/while/body/eval_jaxpr/add | solution.py:84
  231.4 3.3 %add_multiply_fusion = f32[16,40,640]{2,1,0:T(8,128)} fusion(f32[16,40,640]{2,1,0:T(8,128)} %get-tuple-element.265, f32[16,40,640]{2,1,0:T(8,128)} %get-tuple-element.266), kind=kLoop, calls=%fused_computation.27 | loop fusion | flops 819200 | bytes 4915200 | tf_op jit(solution)/shard_map/mul | solution.py:96
  234.7 16.0 %while.34 = (s32[]{:T(128)}, f32[40,640]{1,0:T(8,128)S(1)}, f32[16,40,640]{2,1,0:T(8,128)S(1)}, f32[40]{0:T(128)S(1)}, f32[16,40,640]{2,1,0:T(8,128)}, /*index=5*/s32[]{:T(128)}, s32[]{:T(128)}) while((s32[]{:T(128)}, f32[40,640]{1,0:T(8,128)S(1)}, f32[16,40,640]{2,1,0:T(8,128)S(1)}, f32[40]{0:T(128)S(1)}, ...), condition=%wide.region_3.4_spmd.clone, body=%wide.region_2.3_spmd.clone.sunk | while | flops 76803 | bytes 410203 | solution.py:105
  234.8 1.0 bitcast_dynamic-update-slice_fusion.2
  235.8 1.0 bitcast_dynamic-update-slice_fusion.2
  237.8 1.0 bitcast_dynamic-update-slice_fusion.2
  238.8 1.0 bitcast_dynamic-update-slice_fusion.2
  239.8 1.0 bitcast_dynamic-update-slice_fusion.2
  240.8 1.0 bitcast_dynamic-update-slice_fusion.2
  241.8 1.0 bitcast_dynamic-update-slice_fusion.2
  242.8 1.0 bitcast_dynamic-update-slice_fusion.2
  243.8 1.0 bitcast_dynamic-update-slice_fusion.2
  244.8 1.0 bitcast_dynamic-update-slice_fusion.2
  245.8 1.0 bitcast_dynamic-update-slice_fusion.2
  246.8 1.0 bitcast_dynamic-update-slice_fusion.2
  247.8 1.0 bitcast_dynamic-update-slice_fusion.2
  249.8 1.0 bitcast_dynamic-update-slice_fusion.2
  251.1 19.5 %all_to_all.19 = bf16[16,40,640]{2,1,0:T(8,128)(2,1)S(1)} all-to-all(bf16[16,40,640]{2,1,0:T(8,128)(2,1)S(1)} %subtract_convert_fusion), channel_id=1, replica_groups=mesh['tm'=16,'sector'=8] {'tm'}, dimensions={0} | all-to-all | bytes 1638400 | tf_op jit(solution)/shard_map/all_to_all | solution.py:119
  (52 shorter events, 7.0 us)
Async XLA Ops:
  6.5 5.1 %copy-start = (bf16[1,640,640]{2,1,0:T(8,128)(2,1)S(1)}, bf16[1,640,640]{2,1,0:T(8,128)(2,1)}, u32[]{:S(2)}) copy-start(bf16[1,640,640]{2,1,0:T(8,128)(2,1)} %param.11) | copy-start | bytes 2457604
  6.5 5.1 %copy-start.2 = (bf16[1,1,640,640]{3,2,1,0:T(8,128)(2,1)S(1)}, bf16[1,1,640,640]{3,2,1,0:T(8,128)(2,1)}, u32[]{:S(2)}) copy-start(bf16[1,1,640,640]{3,2,1,0:T(8,128)(2,1)} %param.10) | copy-start | bytes 2457604
  6.5 104.6 %all-gather.2.cloned.1.call-start = ((), (), s32[]{:S(2)}) async-start(), calls=%async_computation.3 | async-start | bytes 13926400 | tf_op jit(solution)/shard_map/all_gather | solution.py:71
  9.7 12.1 %collective-permute-start.1 = (bf16[1,640,640]{2,1,0:T(8,128)(2,1)}, bf16[1,640,640]{2,1,0:T(8,128)(2,1)S(1)}, u32[]{:S(2)}, u32[]{:S(2)}) collective-permute-start(bf16[1,640,640]{2,1,0:T(8,128)(2,1)} %and_select_fusion.1), channel_id=1, source_target_pairs={{1,0},{2,1},{3,2},{4,3},{5,4},{6,5},{7,6},{9,8},{10,9},{11,10},{12... | collective-permute-start | bytes 2457608 | tf_op jit(solution)/shard_map/ppermute | solution.py:10
  14.6 13.9 %collective-permute-start = (bf16[1,640,640]{2,1,0:T(8,128)(2,1)}, bf16[1,640,640]{2,1,0:T(8,128)(2,1)S(1)}, u32[]{:S(2)}, u32[]{:S(2)}) collective-permute-start(bf16[1,640,640]{2,1,0:T(8,128)(2,1)} %fusion.15), channel_id=1, source_target_pairs={{0,1},{1,2},{2,3},{3,4},{4,5},{5,6},{6,7},{8,9},{9,10},{10,11},{11... | collective-permute-start | bytes 2457608 | tf_op jit(solution)/shard_map/ppermute | solution.py:10
  28.4 0.9 copy-start.3
  33.5 16.0 %all-to-all-start = ((bf16[16,1,16,640]{3,2,1,0:T(8,128)(2,1)}), bf16[16,1,16,640]{3,2,1,0:T(8,128)(2,1)S(1)}, u32[]{:S(2)}, u32[]{:S(2)}) async-start(bf16[16,1,16,640]{3,2,1,0:T(8,128)(2,1)} %split.8), calls=%async_computation | async-start | bytes 655360 | tf_op jit(solution)/shard_map/all_to_all | solution.py:37
  49.6 18.6 %all-to-all-start.1 = ((bf16[16,1,24,640]{3,2,1,0:T(8,128)(2,1)}), bf16[16,1,24,640]{3,2,1,0:T(8,128)(2,1)S(1)}, u32[]{:S(2)}, u32[]{:S(2)}) async-start(bf16[16,1,24,640]{3,2,1,0:T(8,128)(2,1)} %split.9), calls=%async_computation.1 | async-start | bytes 983040 | tf_op jit(solution)/shard_map/all_to_all | solution.py:37
  250.8 20.7 %copy-start.1 = (bf16[1,640,640]{2,1,0:T(8,128)(2,1)S(1)}, bf16[1,640,640]{2,1,0:T(8,128)(2,1)}, u32[]{:S(2)}) copy-start(bf16[1,640,640]{2,1,0:T(8,128)(2,1)} %param.11) | copy-start | bytes 2457604
Sparse Core Ops, SparseCore 0:
  9.8 101.2 all-gather.1
where the time goes:
time: 280 us; the launch traced here: 278 us
  waiting for transfers between devices  75.2 us (27%)
  other arithmetic  73.3 us (26%)
  matrix products  64.8 us (23%)
  blocking collectives  19.5 us (7%)
  between operations  15.6 us (6%)
  starting transfers between devices  15 us (5%)
  local copies, waits for them, and re-layouts  14.4 us (5%)
    dot_general x8, matrix products, pair_step(): jnp.einsum('uik,ukl->uil', left, window, preferred_element_type=jnp.float32)  58.4 us
    all_gather x1, waiting for transfers between devices, per_device(): history = lax.all_gather(masked_prop, 'tm', axis=0, tiled=True)  42.9 us
    add x8, other arithmetic, pair_step(): backward + jnp.where((slots < time_count - lag)[:, None, None], product[:...  31.9 us
    all_to_all x2, waiting for transfers between devices, several_exchanges(): lax.all_to_all(share, axis, split_axis=0, concat_axis=0, tiled=True)  22 us
    all_to_all x1, blocking collectives, per_device(): lax.all_to_all(new_rows, 'tm', split_axis=0, concat_axis=1, tiled=True)  19.5 us
    concatenate x1, other arithmetic, per_device(): mirrored = jnp.concatenate([history[::-1], history], 0)  18.6 us
    dynamic_update_slice x16, other arithmetic, per_device(): lax.scan(advance, jnp.zeros((rows_each, states), jnp.float32), convolved)  15.7 us
    rev x1, local copies, waits for them, and re-layouts, per_device(): mirrored = jnp.concatenate([history[::-1], history], 0)  10.8 us
  transfers between devices with their start and end apart: 5, of which 5 were waited for; matrix products, arithmetic and copies ran while one was open for 3% of the time, Pallas kernels for 0%

commit v1 on v0

--- a/solution.py
+++ b/solution.py
@@ -68,7 +68,9 @@
     rows_each = states // lax.axis_size("tm")
     first_row = lax.axis_index("tm") * rows_each
     lag_rows = several_exchanges(self_energy, "tm", 2, 1, 0)
-    history = lax.all_gather(masked_prop, "tm", axis=0, tiled=True)
+    history = jnp.concatenate(
+        lax.all_to_all(jnp.stack([masked_prop] * lax.axis_size("tm")), "tm", 0, 0), axis=0
+    )
     mirrored = jnp.concatenate([history[::-1], history], 0)
     slots = jnp.arange(time_count, dtype=jnp.int32)
     wide_slots = jnp.arange(time_count + 1, dtype=jnp.int32)

time: 280 us -> 462 us (1.65)
  waiting for transfers between devices: 75.2 us -> 244 us
  blocking collectives: 19.5 us -> 37.2 us
  between operations: 15.6 us -> 2.22 us
    all_to_all x0 -> x1, waiting for transfers between devices: none -> 227 us  [per_device(): lax.all_to_all(jnp.stack([masked_prop] * lax.axis_size('tm')), 'tm', 0, 0)]
    all_gather x1 -> x0, waiting for transfers between devices: 42.9 us -> none  [per_device(): history = lax.all_gather(masked_prop, 'tm', axis=0, tiled=True)]
    all_to_all x0 -> x1, blocking collectives: none -> 16 us  [several_exchanges(): lax.all_to_all(share, axis, split_axis=0, concat_axis=0, tiled=True)]
    all_to_all x2 -> x1, waiting for transfers between devices: 22 us -> 9.09 us  [several_exchanges(): lax.all_to_all(share, axis, split_axis=0, concat_axis=0, tiled=True)]
    another operation x0 -> x1, local copies, waits for them, and re-layouts: none -> 6.23 us  [per_device(): jnp.stack([masked_prop] * lax.axis_size('tm'))]
    all_to_all x0 -> x1, starting transfers between devices: none -> 4.95 us  [per_device(): lax.all_to_all(jnp.stack([masked_prop] * lax.axis_size('tm')), 'tm', 0, 0)]
    all_to_all x2 -> x1, starting transfers between devices: 10.7 us -> 7.03 us  [several_exchanges(): lax.all_to_all(share, axis, split_axis=0, concat_axis=0, tiled=True)]
  transfers between devices with their start and end apart: 5 -> 4, of which waited for: 5 -> 4; matrix products, arithmetic and copies ran while one was open for 3% -> 0% of each run, Pallas kernels for 0% -> 0%
where the time goes in v1:
time: 462 us; the launch traced here: 458 us
  waiting for transfers between devices  244 us (53%)
  other arithmetic  72.7 us (16%)
  matrix products  64.7 us (14%)
  blocking collectives  37.2 us (8%)
  local copies, waits for them, and re-layouts  19 us (4%)
  starting transfers between devices  17.5 us (4%)
    all_to_all x1, waiting for transfers between devices, per_device(): lax.all_to_all(jnp.stack([masked_prop] * lax.axis_size('tm')), 'tm', 0, 0)  227 us
    dot_general x8, matrix products, pair_step(): jnp.einsum('uik,ukl->uil', left, window, preferred_element_type=jnp.float32)  58.4 us
    add x8, other arithmetic, pair_step(): backward + jnp.where((slots < time_count - lag)[:, None, None], product[:...  31.9 us
    all_to_all x1, blocking collectives, per_device(): lax.all_to_all(new_rows, 'tm', split_axis=0, concat_axis=1, tiled=True)  21.2 us
    concatenate x1, other arithmetic, per_device(): mirrored = jnp.concatenate([history[::-1], history], 0)  18.6 us
    all_to_all x1, blocking collectives, several_exchanges(): lax.all_to_all(share, axis, split_axis=0, concat_axis=0, tiled=True)  16 us
    dynamic_update_slice x16, other arithmetic, per_device(): lax.scan(advance, jnp.zeros((rows_each, states), jnp.float32), convolved)  15.7 us
    rev x1, local copies, waits for them, and re-layouts, per_device(): mirrored = jnp.concatenate([history[::-1], history], 0)  10.8 us
  transfers between devices with their start and end apart: 4, of which 4 were waited for; matrix products, arithmetic and copies ran while one was open for 0% of the time, Pallas kernels for 0%

profile of v1, /device:TPU:32, one launch (start us, length us, event | category | flops | bytes accessed | tf_op | source)
XLA Modules:
  0.0 458.1 jit_solution(13823455452847331370)
XLA Ops:
  0.7 1.5 fusion.17
  2.2 2.8 fusion.15
  5.0 1.9 collective-permute-start
  7.2 3.6 collective-permute-start.1
  12.2 6.7 %collective-permute-done = bf16[1,640,640]{2,1,0:T(8,128)(2,1)S(1)} collective-permute-done((bf16[1,640,640]{2,1,0:T(8,128)(2,1)}, bf16[1,640,640]{2,1,0:T(8,128)(2,1)S(1)}, u32[]{:S(2)}, u32[]{:S(2)}) %collective-permute-start) | collective-permute-done | bytes 819232 | tf_op jit(solution)/shard_map/ppermute | solution.py:10
  18.9 1.9 collective-permute-done.1
  20.7 3.5 fusion.13
  25.0 7.0 %all-to-all-start = ((bf16[16,1,16,640]{3,2,1,0:T(8,128)(2,1)}), bf16[16,1,16,640]{3,2,1,0:T(8,128)(2,1)S(1)}, u32[]{:S(2)}, u32[]{:S(2)}) async-start(bf16[16,1,16,640]{3,2,1,0:T(8,128)(2,1)} %split.8), calls=%async_computation | async-start | bytes 655360 | tf_op jit(solution)/shard_map/all_to_all | solution.py:37
  32.0 9.1 %all-to-all-done = bf16[16,1,16,640]{3,2,1,0:T(8,128)(2,1)S(1)} async-done(((bf16[16,1,16,640]{3,2,1,0:T(8,128)(2,1)}), bf16[16,1,16,640]{3,2,1,0:T(8,128)(2,1)S(1)}, u32[]{:S(2)}, u32[]{:S(2)}) %all-to-all-start) | async-done | bytes 327712 | tf_op jit(solution)/shard_map/all_to_all | solution.py:37
  41.1 16.0 %all_to_all.24 = bf16[16,1,24,640]{3,2,1,0:T(8,128)(2,1)S(1)} all-to-all(bf16[16,1,24,640]{3,2,1,0:T(8,128)(2,1)S(1)} %split.9), channel_id=1, replica_groups=mesh['tm'=16,'sector'=8] {'tm'}, dimensions={0} | all-to-all | bytes 983040 | tf_op jit(solution)/shard_map/all_to_all | solution.py:37
  57.2 6.2 %stack.5 = bf16[16,1,640,640]{3,2,1,0:T(8,128)(2,1)} broadcast(bf16[640,640]{1,0:T(8,128)(2,1)S(1)} %fusion.17), dimensions={2,3} | broadcast | bytes 13926400 | tf_op jit(solution)/shard_map/stack | solution.py:72
  63.4 5.0 %all-to-all-start.2 = ((bf16[16,1,640,640]{3,2,1,0:T(8,128)(2,1)}), bf16[16,1,640,640]{3,2,1,0:T(8,128)(2,1)}, u32[]{:S(2)}, u32[]{:S(2)}) async-start(bf16[16,1,640,640]{3,2,1,0:T(8,128)(2,1)} %stack.5), calls=%async_computation.2 | async-start | bytes 26214400 | tf_op jit(solution)/shard_map/all_to_all | solution.py:72
  69.4 226.7 %all-to-all-done.2 = bf16[16,1,640,640]{3,2,1,0:T(8,128)(2,1)} async-done(((bf16[16,1,640,640]{3,2,1,0:T(8,128)(2,1)}), bf16[16,1,640,640]{3,2,1,0:T(8,128)(2,1)}, u32[]{:S(2)}, u32[]{:S(2)}) %all-to-all-start.2) | async-done | bytes 13107232 | tf_op jit(solution)/shard_map/all_to_all | solution.py:72
  296.1 10.8 %rev.6 = bf16[16,640,640]{2,1,0:T(8,128)(2,1)} reverse(bf16[16,640,640]{2,1,0:T(8,128)(2,1)} %bitcast.21), dimensions={0} | reverse | bytes 26214400 | tf_op jit(solution)/shard_map/rev | solution.py:74
  306.9 18.6 %pad_maximum_fusion = bf16[32,640,640]{2,1,0:T(8,128)(2,1)} fusion(bf16[16,640,640]{2,1,0:T(8,128)(2,1)} %bitcast.21, bf16[16,640,640]{2,1,0:T(8,128)(2,1)} %rev.6), kind=kLoop, calls=%fused_computation.21 | loop fusion | flops 13107200 | bytes 52428800 | tf_op jit(solution)/shard_map/concatenate | solution.py:74
  325.5 90.8 %while.35 = (s32[]{:T(128)}, f32[16,40,640]{2,1,0:T(8,128)}, f32[16,40,640]{2,1,0:T(8,128)}, bf16[16,40,640]{2,1,0:T(8,128)(2,1)S(1)}, bf16[32,640,640]{2,1,0:T(...) while((s32[]{:T(128)}, f32[16,40,640]{2,1,0:T(8,128)}, ...), condition=%wide.region_1.2_spmd.clone.clone, body=%wide.region_0.1_spmd.clone.clone.sunk | while | flops 559948800 | bytes 25805600 | solution.py:97
  325.6 7.3 %fusion.31 = f32[17,40,640]{2,1,0:T(8,128)S(1)} fusion(bf16[32,640,640]{2,1,0:T(8,128)(2,1)} %get-tuple-element.458, s32[]{:T(128)} %get-tuple-element.444, pred[17]{0:T(512)(128)(4,1)S(1)} %iota_compare_fusion.7, bf16[40,640]{1,0:T(8,128)(2,1)S(1)} %get-tuple-element.428, bf16[40,640]{1,0:T(8,128)(2,1)S(1)} %get-tuple-element.429), kind=kOutput, calls=%fused_computation.5.clone.1 | convolution fusion | flops 557491200 | bytes 15770129 | tf_op jit(solution)/shard_map/while/body/eval_jaxpr/uik,ukl->uil/dot_general | solution.py:85
  332.9 2.3 fusion.32
  335.2 7.3 %fusion.31 = f32[17,40,640]{2,1,0:T(8,128)S(1)} fusion(bf16[32,640,640]{2,1,0:T(8,128)(2,1)} %get-tuple-element.458, s32[]{:T(128)} %get-tuple-element.444, pred[17]{0:T(512)(128)(4,1)S(1)} %iota_compare_fusion.7, bf16[40,640]{1,0:T(8,128)(2,1)S(1)} %get-tuple-element.428, bf16[40,640]{1,0:T(8,128)(2,1)S(1)} %get-tuple-element.429), kind=kOutput, calls=%fused_computation.5.clone.1 | convolution fusion | flops 557491200 | bytes 15770129 | tf_op jit(solution)/shard_map/while/body/eval_jaxpr/uik,ukl->uil/dot_general | solution.py:85
  342.6 4.2 fusion.32
  346.8 7.3 %fusion.31 = f32[17,40,640]{2,1,0:T(8,128)S(1)} fusion(bf16[32,640,640]{2,1,0:T(8,128)(2,1)} %get-tuple-element.458, s32[]{:T(128)} %get-tuple-element.444, pred[17]{0:T(512)(128)(4,1)S(1)} %iota_compare_fusion.7, bf16[40,640]{1,0:T(8,128)(2,1)S(1)} %get-tuple-element.428, bf16[40,640]{1,0:T(8,128)(2,1)S(1)} %get-tuple-element.429), kind=kOutput, calls=%fused_computation.5.clone.1 | convolution fusion | flops 557491200 | bytes 15770129 | tf_op jit(solution)/shard_map/while/body/eval_jaxpr/uik,ukl->uil/dot_general | solution.py:85
  354.1 4.2 fusion.32
  358.4 7.3 %fusion.31 = f32[17,40,640]{2,1,0:T(8,128)S(1)} fusion(bf16[32,640,640]{2,1,0:T(8,128)(2,1)} %get-tuple-element.458, s32[]{:T(128)} %get-tuple-element.444, pred[17]{0:T(512)(128)(4,1)S(1)} %iota_compare_fusion.7, bf16[40,640]{1,0:T(8,128)(2,1)S(1)} %get-tuple-element.428, bf16[40,640]{1,0:T(8,128)(2,1)S(1)} %get-tuple-element.429), kind=kOutput, calls=%fused_computation.5.clone.1 | convolution fusion | flops 557491200 | bytes 15770129 | tf_op jit(solution)/shard_map/while/body/eval_jaxpr/uik,ukl->uil/dot_general | solution.py:85
  365.7 4.2 fusion.32
  370.0 7.3 %fusion.31 = f32[17,40,640]{2,1,0:T(8,128)S(1)} fusion(bf16[32,640,640]{2,1,0:T(8,128)(2,1)} %get-tuple-element.458, s32[]{:T(128)} %get-tuple-element.444, pred[17]{0:T(512)(128)(4,1)S(1)} %iota_compare_fusion.7, bf16[40,640]{1,0:T(8,128)(2,1)S(1)} %get-tuple-element.428, bf16[40,640]{1,0:T(8,128)(2,1)S(1)} %get-tuple-element.429), kind=kOutput, calls=%fused_computation.5.clone.1 | convolution fusion | flops 557491200 | bytes 15770129 | tf_op jit(solution)/shard_map/while/body/eval_jaxpr/uik,ukl->uil/dot_general | solution.py:85
  377.3 4.2 fusion.32
  381.6 7.3 %fusion.31 = f32[17,40,640]{2,1,0:T(8,128)S(1)} fusion(bf16[32,640,640]{2,1,0:T(8,128)(2,1)} %get-tuple-element.458, s32[]{:T(128)} %get-tuple-element.444, pred[17]{0:T(512)(128)(4,1)S(1)} %iota_compare_fusion.7, bf16[40,640]{1,0:T(8,128)(2,1)S(1)} %get-tuple-element.428, bf16[40,640]{1,0:T(8,128)(2,1)S(1)} %get-tuple-element.429), kind=kOutput, calls=%fused_computation.5.clone.1 | convolution fusion | flops 557491200 | bytes 15770129 | tf_op jit(solution)/shard_map/while/body/eval_jaxpr/uik,ukl->uil/dot_general | solution.py:85
  388.9 4.2 fusion.32
  393.1 7.3 %fusion.31 = f32[17,40,640]{2,1,0:T(8,128)S(1)} fusion(bf16[32,640,640]{2,1,0:T(8,128)(2,1)} %get-tuple-element.458, s32[]{:T(128)} %get-tuple-element.444, pred[17]{0:T(512)(128)(4,1)S(1)} %iota_compare_fusion.7, bf16[40,640]{1,0:T(8,128)(2,1)S(1)} %get-tuple-element.428, bf16[40,640]{1,0:T(8,128)(2,1)S(1)} %get-tuple-element.429), kind=kOutput, calls=%fused_computation.5.clone.1 | convolution fusion | flops 557491200 | bytes 15770129 | tf_op jit(solution)/shard_map/while/body/eval_jaxpr/uik,ukl->uil/dot_general | solution.py:85
  400.5 4.2 fusion.32
  404.7 7.3 %fusion.31 = f32[17,40,640]{2,1,0:T(8,128)S(1)} fusion(bf16[32,640,640]{2,1,0:T(8,128)(2,1)} %get-tuple-element.458, s32[]{:T(128)} %get-tuple-element.444, pred[17]{0:T(512)(128)(4,1)S(1)} %iota_compare_fusion.7, bf16[40,640]{1,0:T(8,128)(2,1)S(1)} %get-tuple-element.428, bf16[40,640]{1,0:T(8,128)(2,1)S(1)} %get-tuple-element.429), kind=kOutput, calls=%fused_computation.5.clone.1 | convolution fusion | flops 557491200 | bytes 15770129 | tf_op jit(solution)/shard_map/while/body/eval_jaxpr/uik,ukl->uil/dot_general | solution.py:85
  412.0 4.2 fusion.32
  416.3 3.3 add_multiply_fusion
  419.7 16.0 %while.34 = (s32[]{:T(128)}, f32[40,640]{1,0:T(8,128)S(1)}, f32[16,40,640]{2,1,0:T(8,128)S(1)}, f32[40]{0:T(128)S(1)}, f32[16,40,640]{2,1,0:T(8,128)}, /*index=5*/s32[]{:T(128)}, s32[]{:T(128)}) while((s32[]{:T(128)}, f32[40,640]{1,0:T(8,128)S(1)}, f32[16,40,640]{2,1,0:T(8,128)S(1)}, f32[40]{0:T(128)S(1)}, ...), condition=%wide.region_3.4_spmd.clone, body=%wide.region_2.3_spmd.clone.sunk | while | flops 76803 | bytes 410203 | solution.py:107
  419.7 1.0 bitcast_dynamic-update-slice_fusion.2
  420.7 1.0 bitcast_dynamic-update-slice_fusion.2
  422.7 1.0 bitcast_dynamic-update-slice_fusion.2
  423.7 1.0 bitcast_dynamic-update-slice_fusion.2
  424.7 1.0 bitcast_dynamic-update-slice_fusion.2
  425.7 1.0 bitcast_dynamic-update-slice_fusion.2
  426.7 1.0 bitcast_dynamic-update-slice_fusion.2
  427.7 1.0 bitcast_dynamic-update-slice_fusion.2
  428.7 1.0 bitcast_dynamic-update-slice_fusion.2
  429.7 1.0 bitcast_dynamic-update-slice_fusion.2
  430.7 1.0 bitcast_dynamic-update-slice_fusion.2
  431.7 1.0 bitcast_dynamic-update-slice_fusion.2
  432.7 1.0 bitcast_dynamic-update-slice_fusion.2
  436.0 21.2 %all_to_all.25 = bf16[16,40,640]{2,1,0:T(8,128)(2,1)S(1)} all-to-all(bf16[16,40,640]{2,1,0:T(8,128)(2,1)S(1)} %subtract_convert_fusion), channel_id=1, replica_groups=mesh['tm'=16,'sector'=8] {'tm'}, dimensions={0} | all-to-all | bytes 1638400 | tf_op jit(solution)/shard_map/all_to_all | solution.py:121
  (52 shorter events, 6.6 us)
Async XLA Ops:
  0.0 2.2 copy-start
  2.2 4.7 %copy-start.2 = (bf16[1,1,640,640]{3,2,1,0:T(8,128)(2,1)S(1)}, bf16[1,1,640,640]{3,2,1,0:T(8,128)(2,1)}, u32[]{:S(2)}) copy-start(bf16[1,1,640,640]{3,2,1,0:T(8,128)(2,1)} %param.10) | copy-start | bytes 2457604
  5.0 13.9 %collective-permute-start = (bf16[1,640,640]{2,1,0:T(8,128)(2,1)}, bf16[1,640,640]{2,1,0:T(8,128)(2,1)S(1)}, u32[]{:S(2)}, u32[]{:S(2)}) collective-permute-start(bf16[1,640,640]{2,1,0:T(8,128)(2,1)} %fusion.15), channel_id=1, source_target_pairs={{0,1},{1,2},{2,3},{3,4},{4,5},{5,6},{6,7},{8,9},{9,10},{10,11},{11... | collective-permute-start | bytes 2457608 | tf_op jit(solution)/shard_map/ppermute | solution.py:10
  7.2 13.5 %collective-permute-start.1 = (bf16[1,640,640]{2,1,0:T(8,128)(2,1)S(1)}, bf16[1,640,640]{2,1,0:T(8,128)(2,1)S(1)}, u32[]{:S(2)}, u32[]{:S(2)}) collective-permute-start(bf16[1,640,640]{2,1,0:T(8,128)(2,1)S(1)} %and_select_fusion.1), channel_id=1, source_target_pairs={{1,0},{2,1},{3,2},{4,3},{5,4},{6,5},{7,6},{9,8},{10,9},{11,10},{12... | collective-permute-start | bytes 2457608 | tf_op jit(solution)/shard_map/ppermute | solution.py:10
  18.9 1.9 copy-start.3
  25.0 16.2 %all-to-all-start = ((bf16[16,1,16,640]{3,2,1,0:T(8,128)(2,1)}), bf16[16,1,16,640]{3,2,1,0:T(8,128)(2,1)S(1)}, u32[]{:S(2)}, u32[]{:S(2)}) async-start(bf16[16,1,16,640]{3,2,1,0:T(8,128)(2,1)} %split.8), calls=%async_computation | async-start | bytes 655360 | tf_op jit(solution)/shard_map/all_to_all | solution.py:37
  63.4 232.7 %all-to-all-start.2 = ((bf16[16,1,640,640]{3,2,1,0:T(8,128)(2,1)}), bf16[16,1,640,640]{3,2,1,0:T(8,128)(2,1)}, u32[]{:S(2)}, u32[]{:S(2)}) async-start(bf16[16,1,640,640]{3,2,1,0:T(8,128)(2,1)} %stack.5), calls=%async_computation.2 | async-start | bytes 26214400 | tf_op jit(solution)/shard_map/all_to_all | solution.py:72
  435.7 22.4 %copy-start.1 = (bf16[1,640,640]{2,1,0:T(8,128)(2,1)S(1)}, bf16[1,640,640]{2,1,0:T(8,128)(2,1)}, u32[]{:S(2)}) copy-start(bf16[1,640,640]{2,1,0:T(8,128)(2,1)} %param.11) | copy-start | bytes 2457604
